TPU v7x, 256 devices: a whole 4x4x8 slice. The times are simulated.
256 devices in a mesh: dp: 8 (over y, z_hi), mp: 32 (over z_lo, x, core).
Axes of the slice: x: 4, y: 4, z: 8 (z_hi: 2, z_lo: 4; z = z_hi * 4 + z_lo), core: 2. Of those that a mesh axis runs over, the one named last changes fastest.
Arguments:
- features: bfloat16 [256, 1280, 1024], P('dp', 'mp'), may hold values from -6 to 6
- conv_weight: bfloat16 [1280, 1280], P('mp'), may hold values from -0.15625 to 0.15625
- norm_gain: float32 [1280], replicated, may hold values from 0.25 to 1.75
- norm_bias: float32 [1280], replicated, may hold values from -3 to 3
- logit_vector: float32 [1280], replicated, may hold values from -0.625 to 0.625
- labels: int32 [256], P(('dp', 'mp')), may hold values 0 or 1
Outputs:
- grad_features: float32 [256, 1280, 1024], P('dp', 'mp')
- grad_weight: float32 [1280, 1280], P('mp')
- head_grads: float32 [3, 1280], replicated
- loss: float32 [], replicated
All inputs are finite; a program needn't handle non-finite values. No bound on the sum of `labels` on one device may be relied on, other than what follows from the above.
Results may differ from a plain program's by a relative error of at most 0.0029.
Values may be sent and summed in bfloat16 or wider, within the bound.
A program may use at most 128 MiB of HBM per device.

v0:
```python
import jax
import jax.numpy as jnp
from jax import lax
from jax.sharding import Mesh
from jax.sharding import PartitionSpec as P

GROUPS = 32
MP = ("mp_0", "mp_1", "mp_2")
DP = ("dp_0", "dp_1")
DP_MP = ("dp_0", "dp_1", "mp_0", "mp_1", "mp_2")
norm_eps = 1e-05


def from_everyone(x, axis):
    copies = jnp.broadcast_to(x, (lax.axis_size(axis), *x.shape))
    return lax.all_to_all(copies, axis, split_axis=0, concat_axis=0, tiled=True)


def taken_together(x, axis):
    return from_everyone(x, axis).sum(axis=0)


def head_total(pre, norm_gain, norm_bias, logit_vector, signs):
    images, channels, cell_count = pre.shape
    grouped = pre.reshape(images, GROUPS, channels // GROUPS, cell_count)
    center = jnp.mean(grouped, axis=(2, 3), keepdims=True)
    spread = jnp.mean((grouped - center) ** 2, axis=(2, 3), keepdims=True)
    normed = ((grouped - center) * lax.rsqrt(spread + norm_eps)).reshape(
        images, channels, cell_count
    )
    normed = normed * norm_gain[:, None] + norm_bias[:, None]
    hidden = jax.nn.silu(normed)
    logits = (
        jnp.einsum("c,ncs->n", logit_vector, hidden, precision=lax.Precision.HIGHEST) / cell_count
    )
    margin = jnp.maximum(1.0 - signs * logits, 0.0)
    return jnp.sum(margin * margin)


def shards(features, conv_weight, norm_gain, norm_bias, logit_vector, labels):
    signs = 2.0 * labels.astype(jnp.float32) - 1.0
    weight_full = lax.all_gather(conv_weight, MP, axis=0, tiled=True)
    image_block = lax.all_to_all(features, MP, split_axis=0, concat_axis=1, tiled=True)
    pre = jnp.einsum("io,nis->nos", weight_full, image_block, preferred_element_type=jnp.float32)
    total, pull = jax.vjp(
        lambda p, g, b, h: head_total(p, g, b, h, signs), pre, norm_gain, norm_bias, logit_vector
    )
    grad_pre, grad_gain, grad_bias, grad_vec = pull(jnp.ones((), jnp.float32))
    grad_pre = grad_pre.astype(jnp.bfloat16)
    grad_image = jnp.einsum(
        "io,nos->nis", weight_full, grad_pre, preferred_element_type=jnp.float32
    )
    grad_features = lax.all_to_all(
        grad_image.astype(jnp.bfloat16), MP, split_axis=1, concat_axis=0, tiled=True
    ).astype(jnp.float32)
    weight_term = jnp.einsum(
        "nis,nos->io", image_block, grad_pre, preferred_element_type=jnp.float32
    )
    weight_rows = lax.psum_scatter(weight_term, MP, scatter_dimension=0, tiled=True)
    grad_weight = taken_together(weight_rows, DP)
    small = jnp.stack([grad_gain, grad_bias, grad_vec, jnp.full_like(grad_gain, total)])
    small = lax.psum(small, DP_MP)
    total_sum, head_grads = (small[3, 0], small[:3])
    image_total = pre.shape[0] * lax.axis_size(DP) * lax.axis_size(MP)
    loss = total_sum / image_total
    return (grad_features, grad_weight, head_grads, loss)


def solution(mesh):
    finer = Mesh(mesh.devices.reshape(4, 2, 4, 4, 2), ("dp_0", "dp_1", "mp_0", "mp_1", "mp_2"))
    placed = (P(DP, MP, None), P(MP, None), P(), P(), P(), P(DP_MP))
    return jax.shard_map(
        shards,
        mesh=finer,
        in_specs=placed,
        out_specs=(P(DP, MP, None), P(MP, None), P(), P()),
        check_vma=False,
    )
```

profile of v0, /device:TPU:1, one launch (start us, length us, event | category | flops | bytes accessed | tf_op | source)
XLA Modules:
  0.0 425.3 jit_solution(12105964118553905364)
XLA Ops:
  7.2 0.7 all-gather.2.cloned.1.call-update
  7.9 10.0 %all-to-all-start = ((bf16[32,40,1024]{2,1,0:T(8,128)(2,1)}), bf16[32,40,1024]{2,1,0:T(8,128)(2,1)S(1)}, u32[]{:S(2)}, u32[]{:S(2)}) async-start(bf16[32,40,1024]{2,1,0:T(8,128)(2,1)} %param.6), calls=%async_computation | async-start | bytes 5242880 | tf_op jit(solution)/shard_map/all_to_all | solution.py:43
  17.9 0.0 reduce-scatter.4.cloned.1.call-start
  18.6 74.4 %all-to-all-done = bf16[32,40,1024]{2,1,0:T(8,128)(2,1)S(1)} async-done(((bf16[32,40,1024]{2,1,0:T(8,128)(2,1)}), bf16[32,40,1024]{2,1,0:T(8,128)(2,1)S(1)}, u32[]{:S(2)}, u32[]{:S(2)}) %all-to-all-start) | async-done | bytes 2621472 | tf_op jit(solution)/shard_map/all_to_all | solution.py:43
  93.0 4.4 %all-gather.2.cloned.1.call-done = bf16[1280,1280]{1,0:T(8,128)(2,1)} async-done(((bf16[40,1280]{1,0:T(8,128)(2,1)}), bf16[1280,1280]{1,0:T(8,128)(2,1)}) %all-gather.2.cloned.1.call-update) | async-done | bytes 3276816 | tf_op jit(solution)/shard_map/all_gather | solution.py:42
  97.4 7.3 %fusion.11 = (f32[1280]{0:T(1024)S(1)}, f32[1024,1280]{1,0:T(8,128)}) fusion(bf16[1280,1024]{1,0:T(8,128)(2,1)S(1)} %bitcast.93, bf16[1280,1280]{1,0:T(8,128)(2,1)} %all-gather.2.cloned.1.call-done), kind=kOutput, calls=%fused_computation.31 | convolution fusion | flops 3356752640 | bytes 11146240 | tf_op jit(solution)/shard_map/io,nis->nos/dot_general | solution.py:44
  104.8 0.1 reduce_sum.147
  104.8 0.1 reduce_sum.148
  105.0 0.1 sub.52
  105.0 0.1 sub.53
  105.1 3.1 fusion.2
  108.2 0.1 reduce_sum.150
  108.3 0.1 reduce_sum.151
  108.4 0.1 mul.155
  108.5 0.1 mul.156
  108.6 4.2 multiply_reduce_fusion.1
  112.8 0.6 multiply_reduce_fusion.3
  114.1 5.7 %multiply_reduce_fusion = (f32[1280]{0:T(1024)S(1)}, f32[1280]{0:T(1024)S(1)}, f32[1280]{0:T(1024)S(1)}, f32[1280]{0:T(1024)S(1)}) fusion(f32[1024,1280]{1,0:T(8,128)} %get-tuple-element.13, f32[1280]{0:T(1024)S(1)} %mul.156, f32[1280]{0:T(1024)S(1)} %sub.53, f32[1280]{0:T(1024)S(1)} %copy-done, f32[1280]{0:T(1024)S(1)} %copy-done.1, ...), kind=kLoop, calls=%fused_computation.11 | loop fusion | flops 27520000 | bytes 5288960 | tf_op jit(solution)/shard_map/transpose(jvp())/reduce_sum | solution.py:31
  119.8 0.1 reduce_sum.157
  119.9 0.1 reduce_sum.158
  120.0 0.1 reduce_sum.154
  120.1 0.1 reduce_sum.155
  120.3 0.1 mul.177
  120.3 0.1 mul.178
  120.4 3.1 fusion.4
  123.5 0.1 reduce_sum.160
  123.6 0.1 reduce_sum.161
  123.7 0.1 broadcast_in_dim.11
  123.8 0.1 broadcast_in_dim.24
  123.9 11.6 %convolution_bitcast_fusion = f32[1280,1280]{0,1:T(8,128)} fusion(bf16[1280,1024]{1,0:T(8,128)(2,1)S(1)} %bitcast.94, f32[1024,1280]{1,0:T(8,128)} %get-tuple-element.13, f32[1280]{0:T(1024)S(1)} %broadcast_in_dim.24, f32[1280]{0:T(1024)S(1)} %mul.178, f32[1280]{0:T(1024)S(1)} %copy-done.1, f32[1280]{0:T(1024)S(1)} %mul.156, f32[1280]{0:T(1024)S(1)} %sub.53, ...), kind=kOutput, calls=%fused_computation | convolution fusion | flops 3380346880 | bytes 14453760 | tf_op jit(solution)/shard_map/nis,nos->io/dot_general | solution.py:56
  135.5 8.2 %copy.22 = f32[1280,1280]{1,0:T(8,128)} copy(f32[1280,1280]{0,1:T(8,128)} %convolution_bitcast_fusion) | data formatting | bytes 13107200
  143.7 9.8 %fusion.5 = bf16[1,1280,1024]{1,2,0:T(8,128)(2,1)S(1)} fusion(bf16[1280,1280]{1,0:T(8,128)(2,1)} %all-gather.2.cloned.1.call-done, f32[1024,1280]{1,0:T(8,128)} %get-tuple-element.13, f32[1280]{0:T(1024)S(1)} %broadcast_in_dim.24, f32[1280]{0:T(1024)S(1)} %mul.178, f32[1280]{0:T(1024)S(1)} %copy-done.1, f32[1280]{0:T(1024)S(1)} %mul.156, ...), kind=kOutput, calls=%fused_computation.19 | convolution fusion | flops 3381657600 | bytes 11176960 | tf_op jit(solution)/shard_map/io,nos->nis/dot_general | solution.py:50
  153.5 7.9 %copy.17 = bf16[1,1280,1024]{2,0,1:T(2,128)(2,1)} copy(bf16[1,1280,1024]{1,2,0:T(8,128)(2,1)S(1)} %fusion.5) | data formatting | bytes 5242880 | tf_op jit(solution)/shard_map/convert_element_type | solution.py:54
  161.4 0.5 broadcast.211
  161.9 15.6 %reduce.26 = bf16[1280,1024]{1,0:T(8,128)(2,1)S(1)} reduce(bf16[1280,1,1024]{2,1,0:T(2,128)(2,1)} %bitcast.90, bf16[]{:T(256)} %broadcast.211), dimensions={1}, to_apply=%bitcast.83.reduce_sub_computation | reduce | bytes 5242882
  177.5 2.9 reshape.373
  180.4 78.7 %all_to_all.23 = bf16[32,2,20480]{2,1,0:T(2,128)(2,1)S(1)} all-to-all(bf16[32,2,20480]{2,1,0:T(2,128)(2,1)} %reshape.373), channel_id=1, replica_groups=mesh['dp_0'=4,'dp_1'=2,'mp_0'=4,'mp_1'=4,'mp_2'=2] {'mp_0','mp_1','mp_2'}, dimensions={0} | all-to-all | bytes 5242880 | tf_op jit(solution)/shard_map/all_to_all | solution.py:53
  259.1 43.7 %reduce-scatter.4.cloned.1.call-done = f32[40,1280]{1,0:T(8,128)} async-done(((f32[1280,1280]{1,0:T(8,128)}), f32[40,1280]{1,0:T(8,128)}) %reduce-scatter.4.cloned.1.call-update) | async-done | bytes 204816 | tf_op jit(solution)/shard_map/reduce_scatter | solution.py:59
  302.7 2.2 broadcast_in_dim.26
  305.0 7.4 %all-to-all-start.2 = ((f32[8,40,1280]{2,1,0:T(8,128)}), f32[8,40,1280]{2,1,0:T(8,128)}, u32[]{:S(2)}, u32[]{:S(2)}) async-start(f32[8,40,1280]{2,1,0:T(8,128)} %broadcast_in_dim.26), calls=%async_computation.2 | async-start | bytes 3276800 | tf_op jit(solution)/shard_map/all_to_all | solution.py:16
  312.4 0.1 pad.3.clone
  312.5 0.1 maximum_maximum_fusion
  312.6 87.7 %psum.7 = f32[4,1280]{1,0:T(4,128)S(1)} all-reduce(f32[4,1280]{1,0:T(4,128)S(1)} %maximum_maximum_fusion), channel_id=1, replica_groups=mesh['dp_0'=4,'dp_1'=2,'mp_0'=4,'mp_1'=4,'mp_2'=2] {'dp_0','dp_1','mp_0'..., use_global_device_ids=true, to_apply=%region_15.16 | all-reduce | flops 5120 | bytes 40960 | tf_op jit(solution)/shard_map/psum | solution.py:62
  400.3 0.5 slice.9
  401.5 7.2 %reshape.374 = bf16[1280,1,1024]{2,1,0:T(2,128)(2,1)} reshape(bf16[32,2,20480]{2,1,0:T(2,128)(2,1)S(1)} %all_to_all.23) | data formatting | bytes 5242880
  408.6 3.5 copy.18
  412.2 3.0 convert.1
  415.2 2.2 reduce_sum.162
  (20 shorter events, 0.1 us)
Async XLA Ops:
  7.2 90.3 %all-gather.2.cloned.1.call-start = ((), (), s32[]{:S(2)}) async-start(), calls=%async_computation.4 | async-start | bytes 3379200 | tf_op jit(solution)/shard_map/all_gather | solution.py:42
  7.9 85.1 %all-to-all-start = ((bf16[32,40,1024]{2,1,0:T(8,128)(2,1)}), bf16[32,40,1024]{2,1,0:T(8,128)(2,1)S(1)}, u32[]{:S(2)}, u32[]{:S(2)}) async-start(bf16[32,40,1024]{2,1,0:T(8,128)(2,1)} %param.6), calls=%async_computation | async-start | bytes 5242880 | tf_op jit(solution)/shard_map/all_to_all | solution.py:43
  17.9 284.8 %reduce-scatter.4.cloned.1.call-start = ((), (), s32[]{:S(2)}) async-start(), calls=%async_computation.5 | async-start | bytes 6758400 | tf_op jit(solution)/shard_map/reduce_scatter | solution.py:59
  104.8 3.9 copy-start
  104.8 3.9 copy-start.1
  105.1 7.7 %copy-start.2 = (f32[1280]{0:T(1024)S(1)}, f32[1280]{0:T(1024)}, u32[]{:S(2)}) copy-start(f32[1280]{0:T(1024)} %param.10) | copy-start | bytes 15364
  305.0 110.2 %all-to-all-start.2 = ((f32[8,40,1280]{2,1,0:T(8,128)}), f32[8,40,1280]{2,1,0:T(8,128)}, u32[]{:S(2)}, u32[]{:S(2)}) async-start(f32[8,40,1280]{2,1,0:T(8,128)} %broadcast_in_dim.26), calls=%async_computation.2 | async-start | bytes 3276800 | tf_op jit(solution)/shard_map/all_to_all | solution.py:16
  400.3 11.9 %copy-start.3 = (f32[4,1280]{1,0:T(4,128)}, f32[4,1280]{1,0:T(4,128)S(1)}, u32[]{:S(2)}) copy-start(f32[4,1280]{1,0:T(4,128)S(1)} %psum.7) | copy-start | bytes 61444
Sparse Core Ops, SparseCore 0:
  9.8 87.5 all-gather.1
  143.9 158.8 reduce-scatter.3
where the time goes:
time: 426 us; the launch traced here: 425 us
  blocking collectives  166 us (39%)
  waiting for transfers between devices  123 us (29%)
  other arithmetic  38.1 us (9%)
  local copies, waits for them, and re-layouts  34.1 us (8%)
  matrix products  28.7 us (7%)
  starting transfers between devices  17.5 us (4%)
  between operations  17.3 us (4%)
    psum x1, blocking collectives, shards(): small = lax.psum(small, DP_MP)  87.7 us
    all_to_all x1, blocking collectives, shards(): lax.all_to_all(grad_image.astype(jnp.bfloat16), MP, split_axis=1, concat_...  78.7 us
    all_to_all x1, waiting for transfers between devices, shards(): lax.all_to_all(features, MP, split_axis=0, concat_axis=1, tiled=True)  74.4 us
    reduce_scatter x1, waiting for transfers between devices, shards(): lax.psum_scatter(weight_term, MP, scatter_dimension=0, tiled=True)  43.7 us
    unnamed x12, local copies, waits for them, and re-layouts  18.8 us
    unnamed x1, other arithmetic  15.6 us
    dot_general x1, matrix products, shards(): jnp.einsum('nis,nos->io', image_block, grad_pre, preferred_element_type=j...  11.6 us
    all_to_all x1, starting transfers between devices, shards(): lax.all_to_all(features, MP, split_axis=0, concat_axis=1, tiled=True)  10 us
  transfers between devices with their start and end apart: 4, of which 3 were waited for; matrix products, arithmetic and copies ran while one was open for 12% of the time, Pallas kernels for 0%

commit v1 on v0

--- a/solution.py
+++ b/solution.py
@@ -50,8 +50,14 @@
     grad_image = jnp.einsum(
         "io,nos->nis", weight_full, grad_pre, preferred_element_type=jnp.float32
     )
-    grad_features = lax.all_to_all(
-        grad_image.astype(jnp.bfloat16), MP, split_axis=1, concat_axis=0, tiled=True
+    grad_features = jnp.concatenate(
+        lax.all_to_all(
+            jnp.stack(jnp.split(grad_image.astype(jnp.bfloat16), lax.axis_size(MP), axis=1)),
+            MP,
+            0,
+            0,
+        ),
+        axis=0,
     ).astype(jnp.float32)
     weight_term = jnp.einsum(
         "nis,nos->io", image_block, grad_pre, preferred_element_type=jnp.float32

time: 426 us -> 416 us (0.977)
  local copies, waits for them, and re-layouts: 34.1 us -> 58.2 us
  waiting for transfers between devices: 123 us -> 104 us
  other arithmetic: 38.1 us -> 22.6 us
    another operation x0 -> x35, local copies, waits for them, and re-layouts: none -> 37.9 us  [shards(): jnp.stack(jnp.split(grad_image.astype(jnp.bfloat16), lax.axis_size(MP), a...]
    reduce_scatter x1, waiting for transfers between devices: 43.7 us -> 23.8 us  [shards(): lax.psum_scatter(weight_term, MP, scatter_dimension=0, tiled=True)]
    unnamed x1 -> x0, other arithmetic: 15.6 us -> none
    convert_element_type x1 -> x0, local copies, waits for them, and re-layouts: 7.87 us -> none  [shards(): grad_image.astype(jnp.bfloat16)]
    unnamed x12 -> x68, local copies, waits for them, and re-layouts: 18.8 us -> 16.5 us
  transfers between devices with their start and end apart: 4 -> 4, of which waited for: 3 -> 3; matrix products, arithmetic and copies ran while one was open for 12% -> 14% of each run, Pallas kernels for 0% -> 0%
where the time goes in v1:
time: 416 us; the launch traced here: 415 us
  blocking collectives  166 us (40%)
  waiting for transfers between devices  104 us (25%)
  local copies, waits for them, and re-layouts  58.2 us (14%)
  matrix products  28.7 us (7%)
  other arithmetic  22.6 us (5%)
  starting transfers between devices  17.9 us (4%)
  between operations  17.8 us (4%)
    psum x1, blocking collectives, shards(): small = lax.psum(small, DP_MP)  87.3 us
    all_to_all x1, blocking collectives, shards(): lax.all_to_all(jnp.stack(jnp.split(grad_image.astype(jnp.bfloat16), lax.a...  78.6 us
    all_to_all x1, waiting for transfers between devices, shards(): lax.all_to_all(features, MP, split_axis=0, concat_axis=1, tiled=True)  74.3 us
    another operation x35, local copies, waits for them, and re-layouts, shards(): jnp.stack(jnp.split(grad_image.astype(jnp.bfloat16), lax.axis_size(MP), a...  37.9 us
    reduce_scatter x1, waiting for transfers between devices, shards(): lax.psum_scatter(weight_term, MP, scatter_dimension=0, tiled=True)  23.8 us
    unnamed x68, local copies, waits for them, and re-layouts  16.5 us
    dot_general x1, matrix products, shards(): jnp.einsum('nis,nos->io', image_block, grad_pre, preferred_element_type=j...  11.6 us
    all_to_all x1, starting transfers between devices, shards(): lax.all_to_all(features, MP, split_axis=0, concat_axis=1, tiled=True)  10 us
  transfers between devices with their start and end apart: 4, of which 3 were waited for; matrix products, arithmetic and copies ran while one was open for 14% of the time, Pallas kernels for 0%

profile of v1, /device:TPU:1, one launch (start us, length us, event | category | flops | bytes accessed | tf_op | source)
XLA Modules:
  0.0 414.9 jit_solution(16568277558384576949)
XLA Ops:
  7.9 10.0 %all-to-all-start = ((bf16[32,40,1024]{2,1,0:T(8,128)(2,1)}), bf16[32,40,1024]{2,1,0:T(8,128)(2,1)S(1)}, u32[]{:S(2)}, u32[]{:S(2)}) async-start(bf16[32,40,1024]{2,1,0:T(8,128)(2,1)} %param.6), calls=%async_computation | async-start | bytes 5242880 | tf_op jit(solution)/shard_map/all_to_all | solution.py:43
  18.6 74.3 %all-to-all-done = bf16[32,40,1024]{2,1,0:T(8,128)(2,1)S(1)} async-done(((bf16[32,40,1024]{2,1,0:T(8,128)(2,1)}), bf16[32,40,1024]{2,1,0:T(8,128)(2,1)S(1)}, u32[]{:S(2)}, u32[]{:S(2)}) %all-to-all-start) | async-done | bytes 2621472 | tf_op jit(solution)/shard_map/all_to_all | solution.py:43
  92.9 5.0 %all-gather.2.cloned.1.call-done = bf16[1280,1280]{1,0:T(8,128)(2,1)} async-done(((bf16[40,1280]{1,0:T(8,128)(2,1)}), bf16[1280,1280]{1,0:T(8,128)(2,1)}) %all-gather.2.cloned.1.call-update) | async-done | bytes 3276816 | tf_op jit(solution)/shard_map/all_gather | solution.py:42
  97.9 7.3 %fusion.11 = (f32[1280]{0:T(1024)S(1)}, f32[1024,1280]{1,0:T(8,128)}) fusion(bf16[1280,1024]{1,0:T(8,128)(2,1)S(1)} %bitcast.153, bf16[1280,1280]{1,0:T(8,128)(2,1)} %all-gather.2.cloned.1.call-done), kind=kOutput, calls=%fused_computation.96 | convolution fusion | flops 3356752640 | bytes 11146240 | tf_op jit(solution)/shard_map/io,nis->nos/dot_general | solution.py:44
  105.6 3.1 fusion.2
  109.1 4.2 %multiply_reduce_fusion.1 = f32[1280]{0:T(1024)S(1)} fusion(f32[1024,1280]{1,0:T(8,128)} %get-tuple-element.45, f32[1280]{0:T(1024)S(1)} %copy-done.14, f32[1280]{0:T(1024)S(1)} %copy-done.15, f32[1280]{0:T(1024)S(1)} %mul.156, f32[1280]{0:T(1024)S(1)} %sub.53), kind=kLoop, calls=%fused_computation.13 | loop fusion | flops 11795200 | bytes 5268480 | tf_op jit(solution)/shard_map/jvp(c,ncs->n)/reduce_sum | solution.py:34
  114.6 5.7 %multiply_reduce_fusion = (f32[1280]{0:T(1024)S(1)}, f32[1280]{0:T(1024)S(1)}, f32[1280]{0:T(1024)S(1)}, f32[1280]{0:T(1024)S(1)}) fusion(f32[1024,1280]{1,0:T(8,128)} %get-tuple-element.45, f32[1280]{0:T(1024)S(1)} %mul.156, f32[1280]{0:T(1024)S(1)} %sub.53, f32[1280]{0:T(1024)S(1)} %copy-done.14, f32[1280]{0:T(1024)S(1)} %copy-done.15, ...), kind=kLoop, calls=%fused_computation.11 | loop fusion | flops 27520000 | bytes 5288960 | tf_op jit(solution)/shard_map/transpose(jvp())/reduce_sum | solution.py:31
  120.9 3.1 fusion.4
  124.3 11.6 %convolution_bitcast_fusion = f32[1280,1280]{0,1:T(8,128)} fusion(bf16[1280,1024]{1,0:T(8,128)(2,1)S(1)} %bitcast.154, f32[1024,1280]{1,0:T(8,128)} %get-tuple-element.45, f32[1280]{0:T(1024)S(1)} %broadcast_in_dim.24, f32[1280]{0:T(1024)S(1)} %mul.178, f32[1280]{0:T(1024)S(1)} %copy-done.15, f32[1280]{0:T(1024)S(1)} %mul.156, f32[1280]{0:T(1024)S(1)} %sub.53, ...), kind=kOutput, calls=%fused_computation | convolution fusion | flops 3380346880 | bytes 14453760 | tf_op jit(solution)/shard_map/nis,nos->io/dot_general | solution.py:62
  136.0 8.2 %copy.80 = f32[1280,1280]{1,0:T(8,128)} copy(f32[1280,1280]{0,1:T(8,128)} %convolution_bitcast_fusion) | data formatting | bytes 13107200
  144.2 9.8 %fusion.5 = bf16[1,1280,1024]{1,2,0:T(8,128)(2,1)S(1)} fusion(bf16[1280,1280]{1,0:T(8,128)(2,1)} %all-gather.2.cloned.1.call-done, f32[1024,1280]{1,0:T(8,128)} %get-tuple-element.45, f32[1280]{0:T(1024)S(1)} %broadcast_in_dim.24, f32[1280]{0:T(1024)S(1)} %mul.178, f32[1280]{0:T(1024)S(1)} %copy-done.15, f32[1280]{0:T(1024)S(1)} %mul.156, ...), kind=kOutput, calls=%fused_computation.19 | convolution fusion | flops 3381657600 | bytes 11176960 | tf_op jit(solution)/shard_map/io,nos->nis/dot_general | solution.py:50
  154.0 2.4 slice_bitcast_fusion.19
  156.4 1.1 copy.57
  157.5 1.7 copy.56
  159.1 1.7 copy.55
  160.8 1.7 copy.54
  162.5 1.7 copy.53
  164.2 1.7 copy.52
  165.9 1.7 copy.51
  167.6 1.7 copy.50
  169.3 1.7 copy.49
  171.0 1.7 copy.48
  175.0 3.4 slice_bitcast_fusion
  178.4 1.2 copy.76
  179.6 1.1 copy.75
  180.6 1.1 copy.74
  181.7 1.1 copy.73
  182.8 1.1 copy.72
  183.9 1.1 copy.71
  185.0 1.7 copy.70
  186.7 1.7 copy.69
  188.4 1.7 copy.68
  192.1 0.9 constant_dynamic-update-slice_fusion.31
  193.0 0.9 constant_dynamic-update-slice_fusion.30
  193.9 0.9 constant_dynamic-update-slice_fusion.29
  194.8 0.9 constant_dynamic-update-slice_fusion.28
  195.7 0.9 constant_dynamic-update-slice_fusion.27
  196.6 0.9 constant_dynamic-update-slice_fusion.26
  197.5 0.9 constant_dynamic-update-slice_fusion.25
  198.4 0.9 constant_dynamic-update-slice_fusion.24
  199.3 0.9 constant_dynamic-update-slice_fusion.23
  200.6 78.6 %all_to_all.19 = bf16[32,1,40,1024]{3,2,1,0:T(8,128)(2,1)S(1)} all-to-all(bf16[32,1,40,1024]{3,2,1,0:T(8,128)(2,1)S(1)} %constant_dynamic-update-slice_fusion), channel_id=1, replica_groups=mesh['dp_0'=4,'dp_1'=2,'mp_0'=4,'mp_1'=4,'mp_2'=2] {'mp_0','mp_1','mp_2'}, dimensions={0} | all-to-all | bytes 5242880 | tf_op jit(solution)/shard_map/all_to_all | solution.py:54
  279.2 23.8 %reduce-scatter.4.cloned.1.call-done = f32[40,1280]{1,0:T(8,128)} async-done(((f32[1280,1280]{1,0:T(8,128)}), f32[40,1280]{1,0:T(8,128)}) %reduce-scatter.4.cloned.1.call-update) | async-done | bytes 204816 | tf_op jit(solution)/shard_map/reduce_scatter | solution.py:65
  303.0 2.2 broadcast_in_dim.26
  305.2 7.8 %all-to-all-start.2 = ((f32[8,40,1280]{2,1,0:T(8,128)}), f32[8,40,1280]{2,1,0:T(8,128)}, u32[]{:S(2)}, u32[]{:S(2)}) async-start(f32[8,40,1280]{2,1,0:T(8,128)} %broadcast_in_dim.26), calls=%async_computation.2 | async-start | bytes 3276800 | tf_op jit(solution)/shard_map/all_to_all | solution.py:16
  313.2 87.3 %psum.7 = f32[4,1280]{1,0:T(4,128)S(1)} all-reduce(f32[4,1280]{1,0:T(4,128)S(1)} %maximum_maximum_fusion), channel_id=1, replica_groups=mesh['dp_0'=4,'dp_1'=2,'mp_0'=4,'mp_1'=4,'mp_2'=2] {'dp_0','dp_1','mp_0'..., use_global_device_ids=true, to_apply=%region_15.16 | all-reduce | flops 5120 | bytes 40960 | tf_op jit(solution)/shard_map/psum | solution.py:68
  401.7 3.0 bitcast_convert_fusion
  404.7 2.2 reduce_sum.162
  (108 shorter events, 8.1 us)
Async XLA Ops:
  7.2 90.7 %all-gather.2.cloned.1.call-start = ((), (), s32[]{:S(2)}) async-start(), calls=%async_computation.4 | async-start | bytes 3379200 | tf_op jit(solution)/shard_map/all_gather | solution.py:42
  7.9 85.0 %all-to-all-start = ((bf16[32,40,1024]{2,1,0:T(8,128)(2,1)}), bf16[32,40,1024]{2,1,0:T(8,128)(2,1)S(1)}, u32[]{:S(2)}, u32[]{:S(2)}) async-start(bf16[32,40,1024]{2,1,0:T(8,128)(2,1)} %param.6), calls=%async_computation | async-start | bytes 5242880 | tf_op jit(solution)/shard_map/all_to_all | solution.py:43
  17.9 285.0 %reduce-scatter.4.cloned.1.call-start = ((), (), s32[]{:S(2)}) async-start(), calls=%async_computation.5 | async-start | bytes 6758400 | tf_op jit(solution)/shard_map/reduce_scatter | solution.py:65
  105.2 3.8 copy-start.14
  105.2 3.8 copy-start.15
  108.7 4.6 %copy-start.16 = (f32[1280]{0:T(1024)S(1)}, f32[1280]{0:T(1024)}, u32[]{:S(2)}) copy-start(f32[1280]{0:T(1024)} %param.10) | copy-start | bytes 15364
  178.3 11.8 %copy-start.6 = (bf16[1,1,40,1024]{2,3,1,0:T(8,128)(2,1)S(1)}, bf16[1,1,40,1024]{2,3,1,0:T(8,128)(2,1)}, u32[]{:S(2)}) copy-start(bf16[1,1,40,1024]{2,3,1,0:T(8,128)(2,1)} %get-tuple-element.21) | copy-start | bytes 245764
  178.3 12.6 %copy-start.5 = (bf16[1,1,40,1024]{2,3,1,0:T(8,128)(2,1)S(1)}, bf16[1,1,40,1024]{2,3,1,0:T(8,128)(2,1)}, u32[]{:S(2)}) copy-start(bf16[1,1,40,1024]{2,3,1,0:T(8,128)(2,1)} %get-tuple-element.22) | copy-start | bytes 245764
  178.3 12.7 %copy-start.4 = (bf16[1,1,40,1024]{2,3,1,0:T(8,128)(2,1)S(1)}, bf16[1,1,40,1024]{2,3,1,0:T(8,128)(2,1)}, u32[]{:S(2)}) copy-start(bf16[1,1,40,1024]{2,3,1,0:T(8,128)(2,1)} %get-tuple-element.23) | copy-start | bytes 245764
  178.3 12.9 %copy-start.3 = (bf16[1,1,40,1024]{2,3,1,0:T(8,128)(2,1)S(1)}, bf16[1,1,40,1024]{2,3,1,0:T(8,128)(2,1)}, u32[]{:S(2)}) copy-start(bf16[1,1,40,1024]{2,3,1,0:T(8,128)(2,1)} %get-tuple-element.24) | copy-start | bytes 245764
  178.4 13.0 %copy-start.2 = (bf16[1,1,40,1024]{2,3,1,0:T(8,128)(2,1)S(1)}, bf16[1,1,40,1024]{2,3,1,0:T(8,128)(2,1)}, u32[]{:S(2)}) copy-start(bf16[1,1,40,1024]{2,3,1,0:T(8,128)(2,1)} %get-tuple-element.25) | copy-start | bytes 245764
  178.4 13.1 %copy-start.1 = (bf16[1,1,40,1024]{2,3,1,0:T(8,128)(2,1)S(1)}, bf16[1,1,40,1024]{2,3,1,0:T(8,128)(2,1)}, u32[]{:S(2)}) copy-start(bf16[1,1,40,1024]{2,3,1,0:T(8,128)(2,1)} %get-tuple-element.26) | copy-start | bytes 245764
  178.4 13.2 %copy-start = (bf16[1,1,40,1024]{2,3,1,0:T(8,128)(2,1)S(1)}, bf16[1,1,40,1024]{2,3,1,0:T(8,128)(2,1)}, u32[]{:S(2)}) copy-start(bf16[1,1,40,1024]{2,3,1,0:T(8,128)(2,1)} %get-tuple-element.27) | copy-start | bytes 245764
  182.8 17.4 %copy-start.9 = (bf16[1,1,40,1024]{3,2,1,0:T(8,128)(2,1)S(1)}, bf16[1,1,40,1024]{3,2,1,0:T(8,128)(2,1)}, u32[]{:S(2)}) copy-start(bf16[1,1,40,1024]{3,2,1,0:T(8,128)(2,1)} %copy.54) | copy-start | bytes 245764
  183.9 16.3 %copy-start.8 = (bf16[1,1,40,1024]{3,2,1,0:T(8,128)(2,1)S(1)}, bf16[1,1,40,1024]{3,2,1,0:T(8,128)(2,1)}, u32[]{:S(2)}) copy-start(bf16[1,1,40,1024]{3,2,1,0:T(8,128)(2,1)} %copy.55) | copy-start | bytes 245764
  183.9 16.3 %copy-start.7 = (bf16[1,1,40,1024]{3,2,1,0:T(8,128)(2,1)S(1)}, bf16[1,1,40,1024]{3,2,1,0:T(8,128)(2,1)}, u32[]{:S(2)}) copy-start(bf16[1,1,40,1024]{3,2,1,0:T(8,128)(2,1)} %copy.56) | copy-start | bytes 245764
  190.9 9.5 %copy-start.13 = (bf16[1,1,40,1024]{3,2,1,0:T(8,128)(2,1)S(1)}, bf16[1,1,40,1024]{3,2,1,0:T(8,128)(2,1)}, u32[]{:S(2)}) copy-start(bf16[1,1,40,1024]{3,2,1,0:T(8,128)(2,1)} %copy.67) | copy-start | bytes 245764
  191.0 9.4 %copy-start.12 = (bf16[1,1,40,1024]{3,2,1,0:T(8,128)(2,1)S(1)}, bf16[1,1,40,1024]{3,2,1,0:T(8,128)(2,1)}, u32[]{:S(2)}) copy-start(bf16[1,1,40,1024]{3,2,1,0:T(8,128)(2,1)} %copy.68) | copy-start | bytes 245764
  191.0 9.4 %copy-start.11 = (bf16[1,1,40,1024]{3,2,1,0:T(8,128)(2,1)S(1)}, bf16[1,1,40,1024]{3,2,1,0:T(8,128)(2,1)}, u32[]{:S(2)}) copy-start(bf16[1,1,40,1024]{3,2,1,0:T(8,128)(2,1)} %copy.69) | copy-start | bytes 245764
  191.2 9.3 %copy-start.10 = (bf16[1,1,40,1024]{3,2,1,0:T(8,128)(2,1)S(1)}, bf16[1,1,40,1024]{3,2,1,0:T(8,128)(2,1)}, u32[]{:S(2)}) copy-start(bf16[1,1,40,1024]{3,2,1,0:T(8,128)(2,1)} %copy.70) | copy-start | bytes 245764
  305.2 99.5 %all-to-all-start.2 = ((f32[8,40,1280]{2,1,0:T(8,128)}), f32[8,40,1280]{2,1,0:T(8,128)}, u32[]{:S(2)}, u32[]{:S(2)}) async-start(f32[8,40,1280]{2,1,0:T(8,128)} %broadcast_in_dim.26), calls=%async_computation.2 | async-start | bytes 3276800 | tf_op jit(solution)/shard_map/all_to_all | solution.py:16
  400.5 4.2 %copy-start.17 = (f32[4,1280]{1,0:T(4,128)}, f32[4,1280]{1,0:T(4,128)S(1)}, u32[]{:S(2)}) copy-start(f32[4,1280]{1,0:T(4,128)S(1)} %psum.7) | copy-start | bytes 61444
Sparse Core Ops, SparseCore 0:
  9.8 88.0 all-gather.1
  144.3 158.6 reduce-scatter.3
